TPU v7x, 32 devices: a whole 2x2x4 slice. The times are simulated.
32 devices in a mesh: dp: 2 (over x), seq: 4 (over z), tensor: 4 (over y, core).
Axes of the slice: x: 2, y: 2, z: 4, core: 2. Of those that a mesh axis runs over, the one named last changes fastest.
Arguments:
- tokens: bfloat16 [2, 4, 32, 196, 768], P(None, 'dp', 'seq', 'tensor'), may hold values from -6 to 6
- out_grad: bfloat16 [2, 4, 32, 196, 768], P(None, 'dp', 'seq', 'tensor'), may hold values from -6 to 6
- slot_window: int32 [2, 4, 32], P(None, 'dp', 'seq'), may hold values from 0 to 31, each once within a row
- first_gain: float32 [768], replicated, may hold values from 0.5 to 1.5
- first_shift: float32 [768], replicated, may hold values from -0.3 to 0.3
- triple_weight: bfloat16 [768, 2304], P('tensor'), may hold values from -0.21875 to 0.21875
- triple_bias: float32 [2304], replicated, may hold values from -0.3 to 0.3
- height_table: float32 [27, 64], replicated, may hold values from -0.2 to 0.2
- width_table: float32 [27, 64], replicated, may hold values from -0.2 to 0.2
- output_weight: bfloat16 [768, 768], P('tensor'), may hold values from -1.25 to 1.25
- output_bias: float32 [768], replicated, may hold values from -0.3 to 0.3
- second_gain: float32 [768], replicated, may hold values from 0.5 to 1.5
- second_shift: float32 [768], replicated, may hold values from -0.3 to 0.3
- expand_weight: bfloat16 [768, 3072], P('tensor'), may hold values from -0.21875 to 0.21875
- expand_bias: float32 [3072], replicated, may hold values from -0.3 to 0.3
- shrink_weight: bfloat16 [3072, 768], P('tensor'), may hold values from -0.109375 to 0.109375
- shrink_bias: float32 [768], replicated, may hold values from -0.3 to 0.3
Outputs:
- result: bfloat16 [2, 4, 32, 196, 768], P(None, 'dp', 'seq', 'tensor')
- tokens_gradient: bfloat16 [2, 4, 32, 196, 768], P(None, 'dp', 'seq', 'tensor')
- first_gain_gradient: float32 [768], replicated
- first_shift_gradient: float32 [768], replicated
- triple_weight_gradient: float32 [768, 2304], P('tensor')
- triple_bias_gradient: float32 [2304], replicated
- height_table_gradient: float32 [27, 64], replicated
- width_table_gradient: float32 [27, 64], replicated
- output_weight_gradient: float32 [768, 768], P('tensor')
- output_bias_gradient: float32 [768], replicated
- second_gain_gradient: float32 [768], replicated
- second_shift_gradient: float32 [768], replicated
- expand_weight_gradient: float32 [768, 3072], P('tensor')
- expand_bias_gradient: float32 [3072], replicated
- shrink_weight_gradient: float32 [3072, 768], P('tensor')
- shrink_bias_gradient: float32 [768], replicated
Inputs may be any that keep to these rules, and one draw needn't show every extreme that they name: For each micro-batch and image, slot_window is a permutation of 0 to 31; a value w below 25 names the window in row w // 5 and column w % 5 of the grid padded to 70 tokens a side, larger values mark empty slots.
All inputs are finite; a program needn't handle non-finite values.
Results may differ from a plain program's by a relative error of at most 0.015.
Values may be sent and summed in bfloat16 or wider, within the bound.
No kernel may reach another device: no remote copies, remote signals or barrier semaphores. Data moves between devices by JAX's collectives and lax.ppermute only.
A program may use at most 320 MiB of HBM per device.

v0:
```python
import jax
import jax.numpy as jnp
import numpy as np
from jax import lax
from jax.sharding import PartitionSpec as P

HEADS = 12
HD = 64
WIN = 14
GRID = 64
WGRID = 5
EPSILON = 1e-06
MASKED_SCORE = -1000000000.0
PRECISE = lax.Precision.HIGHEST


def layer_norm(values, gain, shift):
    centre = jnp.mean(values, axis=-1, keepdims=True)
    spread = values - centre
    variance = jnp.mean(spread * spread, axis=-1, keepdims=True)
    return spread * lax.rsqrt(variance + EPSILON) * gain + shift


def smooth_gate(values):
    return 0.5 * values * (1.0 + jax.scipy.special.erf(values * 0.7071067811865476))


def window_valid(slot_window, window, grid, across):
    position = jnp.arange(window * window, dtype=jnp.int32)
    window_id = slot_window[..., None]
    inside = (
        (window_id < across * across)
        & (window_id // across * window + position // window < grid)
        & (window_id % across * window + position % window < grid)
    )
    return jnp.where(inside, 1.0, 0.0).astype(jnp.float32)


def offset_table(window):
    first_index = np.arange(window)[:, None, None]
    second = np.arange(window)[None, :, None]
    offset = np.arange(2 * window - 1)[None, None, :]
    return jnp.asarray((first_index - second + window - 1 == offset).astype(np.float32))


def key_expanders(window):
    positions = np.arange(window * window)[None, :]
    sides = np.arange(window)[:, None]
    by_height = jnp.asarray((positions // window == sides).astype(np.float32))
    by_width = jnp.asarray((positions % window == sides).astype(np.float32))
    return (by_height, by_width)


def contract_rows(left, right):
    return lax.dot_general(
        left, right, (((0,), (0,)), ((), ())), preferred_element_type=jnp.float32
    )


def times_transposed(left, weight):
    return lax.dot_general(
        left, weight, (((1,), (1,)), ((), ())), preferred_element_type=jnp.float32
    )


def scores_of(query_rows, key_rows, height_full, width_full, valid_keys):
    slab_count, full_rows, heads_dev, head_dim = query_rows.shape
    window = height_full.shape[0]
    by_height, by_width = key_expanders(window)
    raw_scores = jnp.einsum(
        "sqhc,skhc->shqk", query_rows, key_rows, preferred_element_type=jnp.float32
    ) * head_dim ** (-0.5)
    grid_query = query_rows.astype(jnp.float32).reshape(
        slab_count, window, window, heads_dev, head_dim
    )
    along_height = jnp.einsum("sijhc,ikc->shijk", grid_query, height_full, precision=PRECISE)
    along_width = jnp.einsum("sijhc,jlc->shijl", grid_query, width_full, precision=PRECISE)
    along_height = along_height.reshape(slab_count, heads_dev, full_rows, window)
    along_width = along_width.reshape(slab_count, heads_dev, full_rows, window)
    height_bias = jnp.einsum("shqk,kc->shqc", along_height, by_height, precision=PRECISE)
    width_bias = jnp.einsum("shql,lc->shqc", along_width, by_width, precision=PRECISE)
    summed = raw_scores + height_bias + width_bias
    return (jnp.where(valid_keys[:, None, None, :] > 0, summed, MASKED_SCORE), grid_query)


def attend(heads, valid_full, height_full, width_full):
    masked, grid_query = scores_of(
        heads[:, :, 0], heads[:, :, 1], height_full, width_full, valid_full
    )
    maxima = jnp.max(masked, axis=-1, keepdims=True)
    exponent = jnp.exp(masked - maxima)
    summed = jnp.sum(exponent, axis=-1, keepdims=True)
    soft_low = (exponent / summed).astype(jnp.bfloat16)
    mixed_rows = jnp.einsum(
        "shqk,skhc->sqhc", soft_low, heads[:, :, 2], preferred_element_type=jnp.float32
    )
    mixed_rows = mixed_rows * valid_full[:, :, None, None]
    slab_count, full_rows, heads_dev, head_dim = mixed_rows.shape
    packed_rows = mixed_rows.astype(jnp.bfloat16).reshape(
        slab_count, full_rows, 1, heads_dev * head_dim
    )
    return (packed_rows, maxima + jnp.log(summed))


def attend_back(heads, valid_full, height_full, width_full, offsets, log_total, grad_mixed):
    query_rows = heads[:, :, 0]
    key_rows = heads[:, :, 1]
    value_rows = heads[:, :, 2]
    slab_count, full_rows, heads_dev, head_dim = query_rows.shape
    window = height_full.shape[0]
    by_height, by_width = key_expanders(window)
    masked, grid_query = scores_of(query_rows, key_rows, height_full, width_full, valid_full)
    soft_weights = jnp.exp(masked - log_total)
    soft_low = soft_weights.astype(jnp.bfloat16)
    grad_out = grad_mixed * valid_full[:, :, None, None].astype(jnp.bfloat16)
    grad_values = jnp.einsum(
        "shqk,sqhc->skhc", soft_low, grad_out, preferred_element_type=jnp.float32
    )
    grad_soft = jnp.einsum(
        "sqhc,skhc->shqk", grad_out, value_rows, preferred_element_type=jnp.float32
    )
    grad_scores = soft_weights * (
        grad_soft - jnp.sum(soft_weights * grad_soft, axis=-1, keepdims=True)
    )
    grad_scores = jnp.where(valid_full[:, None, None, :] > 0, grad_scores, 0.0).astype(jnp.bfloat16)
    score_scale = head_dim ** (-0.5)
    grad_queries = (
        jnp.einsum("shqk,skhc->sqhc", grad_scores, key_rows, preferred_element_type=jnp.float32)
        * score_scale
    )
    grad_keys = (
        jnp.einsum("shqk,sqhc->skhc", grad_scores, query_rows, preferred_element_type=jnp.float32)
        * score_scale
    )
    grad_wide = grad_scores.astype(jnp.float32)
    grad_height = jnp.einsum("shqc,kc->shqk", grad_wide, by_height, precision=PRECISE)
    grad_width = jnp.einsum("shqc,lc->shql", grad_wide, by_width, precision=PRECISE)
    grad_height = grad_height.reshape(slab_count, heads_dev, window, window, window)
    grad_width = grad_width.reshape(slab_count, heads_dev, window, window, window)
    grid_query_grad = jnp.einsum("shijk,ikc->sijhc", grad_height, height_full, precision=PRECISE)
    grid_query_grad = grid_query_grad + jnp.einsum(
        "shijl,jlc->sijhc", grad_width, width_full, precision=PRECISE
    )
    grad_queries = grad_queries + grid_query_grad.reshape(
        slab_count, full_rows, heads_dev, head_dim
    )
    height_expanded = jnp.einsum("shijk,sijhc->ikc", grad_height, grid_query, precision=PRECISE)
    width_expanded = jnp.einsum("shijl,sijhc->jlc", grad_width, grid_query, precision=PRECISE)
    height_grad = jnp.einsum("ikr,ikc->rc", offsets, height_expanded, precision=PRECISE)
    width_grad = jnp.einsum("ikr,ikc->rc", offsets, width_expanded, precision=PRECISE)
    grad_heads = jnp.stack((grad_queries, grad_keys, grad_values), axis=2).astype(jnp.bfloat16)
    return (
        grad_heads.reshape(slab_count, full_rows, 3, 1, heads_dev * head_dim),
        height_grad,
        width_grad,
    )


def local(
    tokens,
    out_grad,
    slot_window,
    first_gain,
    first_shift,
    triple_weight,
    triple_bias,
    height_table,
    width_table,
    output_weight,
    output_bias,
    second_gain,
    second_shift,
    expand_weight,
    expand_bias,
    shrink_weight,
    shrink_bias,
):
    micro_count, images, slot_dev, rows_dev, model_width = tokens.shape
    tensor_parts = lax.axis_size("tensor")
    heads_dev = HEADS // tensor_parts
    head_width = heads_dev * HD
    full_rows = rows_dev * tensor_parts
    slab_count = images * slot_dev
    row_count = slab_count * rows_dev
    offsets = offset_table(WIN)
    height_full = jnp.einsum("ikr,rc->ikc", offsets, height_table, precision=PRECISE)
    width_full = jnp.einsum("ikr,rc->ikc", offsets, width_table, precision=PRECISE)
    triple_full, output_full, expand_full, shrink_full = (
        lax.all_gather(triple_weight, "tensor", axis=0, tiled=True),
        lax.all_gather(output_weight, "tensor", axis=0, tiled=True),
        lax.all_gather(expand_weight, "tensor", axis=0, tiled=True),
        lax.all_gather(shrink_weight, "tensor", axis=0, tiled=True),
    )
    first_row = lax.axis_index("tensor") * rows_dev
    sums = [
        jnp.zeros(item.shape, jnp.float32)
        for item in (
            first_gain,
            first_shift,
            triple_full,
            triple_bias,
            height_table,
            width_table,
            output_full,
            output_bias,
            second_gain,
            second_shift,
            expand_full,
            expand_bias,
            shrink_full,
            shrink_bias,
        )
    ]
    results = []
    input_grads = []
    for micro_step in range(micro_count):
        valid_full = window_valid(slot_window[micro_step], WIN, GRID, WGRID).reshape(
            slab_count, full_rows
        )
        valid_local = lax.dynamic_slice_in_dim(valid_full, first_row, rows_dev, axis=1).reshape(
            row_count, 1
        )
        row_values = tokens[micro_step].astype(jnp.float32).reshape(row_count, model_width)
        normed = layer_norm(row_values, first_gain, first_shift).astype(jnp.bfloat16)
        triple = (
            jnp.dot(normed, triple_full, preferred_element_type=jnp.float32) + triple_bias
        ).astype(jnp.bfloat16)
        triple = triple.reshape(slab_count, rows_dev, 3, tensor_parts, head_width)
        heads = lax.all_to_all(triple, "tensor", split_axis=3, concat_axis=1, tiled=True)
        heads = heads.reshape(slab_count, full_rows, 3, heads_dev, HD)
        mixed_rows, log_total = attend(heads, valid_full, height_full, width_full)
        attended = lax.all_to_all(
            mixed_rows, "tensor", split_axis=1, concat_axis=2, tiled=True
        ).reshape(row_count, model_width)
        middle = (
            row_values
            + jnp.dot(attended, output_full, preferred_element_type=jnp.float32)
            + output_bias
        )
        normed2 = layer_norm(middle, second_gain, second_shift).astype(jnp.bfloat16)
        hidden = jnp.dot(normed2, expand_full, preferred_element_type=jnp.float32) + expand_bias
        active = smooth_gate(hidden).astype(jnp.bfloat16)
        output_rows = (
            middle + jnp.dot(active, shrink_full, preferred_element_type=jnp.float32) + shrink_bias
        )
        results.append(
            output_rows.astype(jnp.bfloat16).reshape(images, slot_dev, rows_dev, model_width)
        )
        grad_result = (
            out_grad[micro_step].astype(jnp.float32).reshape(row_count, model_width) * valid_local
        )
        grad_branch = grad_result.astype(jnp.bfloat16)
        sums[12] = sums[12] + contract_rows(active, grad_branch)
        sums[13] = sums[13] + jnp.sum(grad_branch, axis=0, dtype=jnp.float32)
        grad_active = times_transposed(grad_branch, shrink_full)
        unused_value, gate_back = jax.vjp(smooth_gate, hidden)
        grad_hidden = gate_back(grad_active)[0].astype(jnp.bfloat16)
        sums[10] = sums[10] + contract_rows(normed2, grad_hidden)
        sums[11] = sums[11] + jnp.sum(grad_hidden, axis=0, dtype=jnp.float32)
        grad_normed2 = times_transposed(grad_hidden, expand_full)
        unused_value, second_back = jax.vjp(layer_norm, middle, second_gain, second_shift)
        grad_middle, grad_gain, grad_shift = second_back(grad_normed2)
        sums[8] = sums[8] + grad_gain
        sums[9] = sums[9] + grad_shift
        grad_middle = grad_result + grad_middle
        grad_output = grad_middle.astype(jnp.bfloat16)
        sums[6] = sums[6] + contract_rows(attended, grad_output)
        sums[7] = sums[7] + jnp.sum(grad_output, axis=0, dtype=jnp.float32)
        grad_attended = times_transposed(grad_output, output_full).astype(jnp.bfloat16)
        grad_attended = grad_attended.reshape(slab_count, rows_dev, tensor_parts, head_width)
        grad_mixed = lax.all_to_all(
            grad_attended, "tensor", split_axis=2, concat_axis=1, tiled=True
        )
        grad_mixed = grad_mixed.reshape(slab_count, full_rows, heads_dev, HD)
        grad_heads, height_grad, width_grad = attend_back(
            heads, valid_full, height_full, width_full, offsets, log_total, grad_mixed
        )
        sums[4] = sums[4] + height_grad
        sums[5] = sums[5] + width_grad
        grad_triple = lax.all_to_all(
            grad_heads, "tensor", split_axis=1, concat_axis=3, tiled=True
        ).reshape(row_count, 3 * model_width)
        sums[2] = sums[2] + contract_rows(normed, grad_triple)
        sums[3] = sums[3] + jnp.sum(grad_triple, axis=0, dtype=jnp.float32)
        grad_normed = times_transposed(grad_triple, triple_full)
        unused_value, first_back = jax.vjp(layer_norm, row_values, first_gain, first_shift)
        grad_rows, grad_gain, grad_shift = first_back(grad_normed)
        sums[0] = sums[0] + grad_gain
        sums[1] = sums[1] + grad_shift
        grad_input = (grad_middle + grad_rows).astype(jnp.bfloat16)
        input_grads.append(grad_input.reshape(images, slot_dev, rows_dev, model_width))
    shares = (
        lax.psum_scatter(
            sums[2].astype(jnp.bfloat16), "tensor", scatter_dimension=0, tiled=True
        ).astype(jnp.float32),
        lax.psum_scatter(
            sums[6].astype(jnp.bfloat16), "tensor", scatter_dimension=0, tiled=True
        ).astype(jnp.float32),
        lax.psum_scatter(
            sums[10].astype(jnp.bfloat16), "tensor", scatter_dimension=0, tiled=True
        ).astype(jnp.float32),
        lax.psum_scatter(
            sums[12].astype(jnp.bfloat16), "tensor", scatter_dimension=0, tiled=True
        ).astype(jnp.float32),
    )
    blocks = lax.psum((shares[0], shares[1], shares[2], shares[3]), ("dp", "seq"))
    triple_gradient = blocks[0]
    output_gradient = blocks[1]
    expand_gradient = blocks[2]
    shrink_gradient = blocks[3]
    small = lax.psum(
        (
            sums[0],
            sums[1],
            sums[3],
            sums[4],
            sums[5],
            sums[7],
            sums[8],
            sums[9],
            sums[11],
            sums[13],
        ),
        ("dp", "seq", "tensor"),
    )
    result = jnp.stack(results, axis=0)
    tokens_gradient = jnp.stack(input_grads, axis=0)
    return (
        result,
        tokens_gradient,
        small[0],
        small[1],
        triple_gradient,
        small[2],
        small[3],
        small[4],
        output_gradient,
        small[5],
        small[6],
        small[7],
        expand_gradient,
        small[8],
        shrink_gradient,
        small[9],
    )


def solution(mesh):
    return jax.shard_map(
        local,
        mesh=mesh,
        in_specs=(
            P(None, "dp", "seq", "tensor", None),
            P(None, "dp", "seq", "tensor", None),
            P(None, "dp", "seq"),
            P(),
            P(),
            P("tensor", None),
            P(),
            P(),
            P(),
            P("tensor", None),
            P(),
            P(),
            P(),
            P("tensor", None),
            P(),
            P("tensor", None),
            P(),
        ),
        out_specs=(
            P(None, "dp", "seq", "tensor", None),
            P(None, "dp", "seq", "tensor", None),
            P(),
            P(),
            P("tensor", None),
            P(),
            P(),
            P(),
            P("tensor", None),
            P(),
            P(),
            P(),
            P("tensor", None),
            P(),
            P("tensor", None),
            P(),
        ),
        check_vma=False,
    )
```

profile of v0, /device:TPU:0, one launch (start us, length us, event | category | flops | bytes accessed | tf_op | source)
XLA Modules:
  0.0 1686.3 jit_solution(17513940450612606039)
XLA Ops:
  17.8 25.3 %all-gather.5.cloned.1.call-done = bf16[768,2304]{1,0:T(8,128)(2,1)} async-done(((bf16[192,2304]{1,0:T(8,128)(2,1)}), bf16[768,2304]{1,0:T(8,128)(2,1)}) %all-gather.5.cloned.1.call-update) | async-done | bytes 3538960 | tf_op jit(solution)/shard_map/all_gather | solution.py:189
  50.8 10.1 reshape.1058
  85.2 10.1 reshape.1065
  100.4 63.5 %all-to-all-done = bf16[16,49,3,4,192]{4,0,2,1,3:T(8,128)(2,1)} async-done(((bf16[16,49,3,4,192]{4,0,2,1,3:T(8,128)(2,1)}), bf16[16,49,3,4,192]{4,0,2,1,3:T(8,128)(2,1)}, u32[]{:S(2)}, u32[]{:S(2)}) %all-to-all-start) | async-done | bytes 3612704 | tf_op jit(solution)/shard_map/all_to_all | solution.py:229
  171.0 18.2 %reshape.1102 = bf16[16,196,3,3,64]{4,3,0,2,1:T(4,128)(2,1)} reshape(bf16[16,4,49,3,1,192]{5,0,3,2,1,4:T(8,128)(2,1)} %bitcast.1) | data formatting | bytes 7225344 | tf_op jit(solution)/shard_map/reshape | solution.py:230
  189.2 10.0 fusion.166
  208.0 20.2 %all-to-all-done.2 = bf16[16,49,3,4,192]{4,0,2,1,3:T(8,128)(2,1)} async-done(((bf16[16,49,3,4,192]{4,0,2,1,3:T(8,128)(2,1)}), bf16[16,49,3,4,192]{4,0,2,1,3:T(8,128)(2,1)}, u32[]{:S(2)}, u32[]{:S(2)}) %all-to-all-start.2) | async-done | bytes 3612704 | tf_op jit(solution)/shard_map/all_to_all | solution.py:229
  228.2 18.2 %reshape.1104 = bf16[16,196,3,3,64]{4,3,0,2,1:T(4,128)(2,1)} reshape(bf16[16,4,49,3,1,192]{5,0,3,2,1,4:T(8,128)(2,1)} %bitcast.25) | data formatting | bytes 7225344 | tf_op jit(solution)/shard_map/reshape | solution.py:230
  246.4 10.9 fusion.167
  265.5 19.1 %fusion.52 = f32[16,3,14,14,14]{0,4,1,2,3:T(8,128)} fusion(bf16[16,14,14,3,64]{4,0,3,2,1:T(8,128)(2,1)S(1)} %bitcast.281, f32[14,14,64]{2,1,0:T(8,128)S(1)} %fusion.128), kind=kOutput, calls=%fused_computation.124 | convolution fusion | flops 101154816 | bytes 1781248 | tf_op jit(solution)/shard_map/sijhc,jlc->shijl/dot_general | solution.py:77
  284.6 19.2 %fusion.170 = f32[14,14,16,14,3]{2,1,4,3,0:T(8,128)} fusion(f32[14,14,64,1,1]{2,1,4,3,0:T(8,128)S(1)} %convolution_bitcast_fusion, bf16[16,14,14,3,64]{4,0,3,2,1:T(8,128)(2,1)S(1)} %bitcast.282), kind=kOutput, calls=%fused_computation.272 | convolution fusion | flops 101154816 | bytes 1781248 | tf_op jit(solution)/shard_map/sijhc,ikc->shijk/dot_general | solution.py:76
  303.8 19.1 %fusion.55 = f32[16,3,14,14,14]{0,4,1,2,3:T(8,128)} fusion(bf16[16,14,14,3,64]{4,0,3,2,1:T(8,128)(2,1)S(1)} %bitcast.285, f32[14,14,64]{2,1,0:T(8,128)S(1)} %fusion.128), kind=kOutput, calls=%fused_computation.125 | convolution fusion | flops 101154816 | bytes 1781248 | tf_op jit(solution)/shard_map/sijhc,jlc->shijl/dot_general | solution.py:77
  322.9 19.4 %fusion.173 = f32[14,14,16,14,3]{2,1,4,3,0:T(8,128)} fusion(f32[14,14,64,1,1]{2,1,4,3,0:T(8,128)S(1)} %convolution_bitcast_fusion, bf16[16,14,14,3,64]{4,0,3,2,1:T(8,128)(2,1)S(1)} %bitcast.286), kind=kOutput, calls=%fused_computation.275 | convolution fusion | flops 101154816 | bytes 1781248 | tf_op jit(solution)/shard_map/sijhc,ikc->shijk/dot_general | solution.py:76
  347.2 9.8 copy.430
  377.0 9.8 copy.435
  396.3 11.4 fusion.174
  407.8 12.1 copy.353
  419.9 11.3 fusion.175
  431.1 12.0 copy.357
  443.2 11.3 fusion.171
  454.5 12.2 copy.333
  466.7 11.4 fusion.172
  478.0 12.1 copy.337
  496.7 12.1 copy.350
  514.0 12.0 copy.330
  526.1 26.2 %fusion.164 = (f32[16,3,196]{0,2,1:T(8,128)S(1)}, f32[16,3,196,196]{3,0,2,1:T(8,128)}, f32[16,3,196]{0,2,1:T(8,128)S(1)}, f32[16,3,196,196]{3,0,2,1:T(8,128)}) fusion(f32[16,3,196,196]{3,0,2,1:T(8,128)} %copy.337, f32[16,3,196,196]{3,0,2,1:T(8,128)} %copy.333, f32[16,3,196,196]{3,0,2,1:T(8,128)} %copy.330, pred[16,196]{1,0:T(8,128)(4,1)S(1)} %get-tuple-element.166, ...), kind=kLoop, calls=%fused_computation.266 | loop fusion | flops 18420864 | bytes 59088512 | tf_op jit(solution)/shard_map/reduce_max | solution.py:90
  581.4 9.5 fusion.6
  644.3 10.7 fusion.159
  655.1 14.6 convert_reduce_fusion
  675.9 11.5 multiply_convert_fusion.1
  687.4 15.4 convert_reduce_fusion.1
  702.9 9.4 multiply_reduce_fusion.3
  730.7 9.5 add_convert_fusion.3
  825.0 12.4 copy.365
  837.4 62.1 %select_convert_fusion.1 = bf16[16,3,196,196]{3,0,2,1:T(8,128)(2,1)S(1)} fusion(f32[16,3,196,196]{3,0,2,1:T(8,128)} %copy.365, f32[16,3,196,196]{3,0,2,1:T(8,128)} %get-tuple-element.125, f32[16,3,196]{0,2,1:T(8,128)S(1)} %copy-done.65, pred[16,196]{1,0:T(8,128)(4,1)S(1)} %copy-done.88), kind=kOutput, calls=%fused_computation.11 | output fusion | flops 12917379 | bytes 18480448 | tf_op jit(solution)/shard_map/sub | solution.py:123
  966.4 11.5 fusion.176
  1028.2 12.1 copy.385
  1040.3 62.0 %select_convert_fusion = bf16[16,3,196,196]{3,0,2,1:T(8,128)(2,1)S(1)} fusion(f32[16,3,196,196]{3,0,2,1:T(8,128)} %copy.385, f32[16,3,196,196]{3,0,2,1:T(8,128)} %get-tuple-element.192, f32[16,3,196]{0,2,1:T(8,128)S(1)} %copy-done.63, pred[16,196]{1,0:T(8,128)(4,1)S(1)} %copy-done.86), kind=kOutput, calls=%fused_computation.6 | output fusion | flops 12917379 | bytes 18480448 | tf_op jit(solution)/shard_map/sub | solution.py:123
  1152.6 10.1 fusion.178
  1199.5 8.7 add_convert_fusion.11
  1210.8 8.7 add_convert_fusion.14
  1230.6 8.9 reshape.1077
  1239.6 13.0 all-to-all-done.7
  1259.6 9.5 reshape.1083
  1289.5 9.4 copy.410
  1298.9 9.7 copy.412
  1360.1 41.9 %all-reduce = (f32[768]{0:T(1024)}, f32[768]{0:T(1024)}, f32[2304]{0:T(1024)}, f32[27,64]{1,0:T(8,128)}, f32[27,64]{1,0:T(8,128)}, /*index=5*/f32[768]{0:T(1024)...) all-reduce(f32[768]{0:T(1024)S(1)} %add.540, ...), channel_id=1, replica_groups=mesh['dp'=2,'seq'=4,'tensor'=4] {'dp','seq','tensor'}, use_global_device_ids=true, to_apply=%region_24.25 | all-reduce | flops 13440 | bytes 107520 | tf_op jit(solution)/shard_map/psum | solution.py:311
  1402.1 277.1 %all-reduce.3 = (f32[192,2304]{1,0:T(8,128)}, f32[192,768]{1,0:T(8,128)}, f32[192,3072]{1,0:T(8,128)}, f32[768,768]{1,0:T(8,128)}) all-reduce(bf16[192,2304]{1,0:T(8,128)(2,1)} %reduce-scatter.5.cloned.1.call-done, bf16[192,768]{1,0:T(8,128)(2,1)S(1)} %copy-done.76, ...), channel_id=1, replica_groups=mesh['dp'=2,'seq'=4,'tensor'=4] {'dp','seq'}, use_global_device_ids=true, to_apply=%region_29.30 | all-reduce | flops 1769472 | bytes 10616832 | tf_op jit(solution)/shard_map/psum | solution.py:306
  (513 shorter events, 605.2 us)
Async XLA Ops:
  7.2 162.4 %copy-start = (f32[27,64]{1,0:T(8,128)S(1)}, f32[27,64]{1,0:T(8,128)}, u32[]{:S(2)}) copy-start(f32[27,64]{1,0:T(8,128)} %param.37) | copy-start | bytes 20740
  7.2 35.9 %all-gather.5.cloned.1.call-start = ((), (), s32[]{:S(2)}) async-start(), calls=%async_computation.12 | async-start | bytes 4423680 | tf_op jit(solution)/shard_map/all_gather | solution.py:189
  7.9 628.7 %all-gather.7.cloned.1.call-start = ((), (), s32[]{:S(2)}) async-start(), calls=%async_computation.13 | async-start | bytes 1474560 | tf_op jit(solution)/shard_map/all_gather | solution.py:190
  8.7 635.4 %all-gather.9.cloned.1.call-start = ((), (), s32[]{:S(2)}) async-start(), calls=%async_computation.14 | async-start | bytes 5898240 | tf_op jit(solution)/shard_map/all_gather | solution.py:191
  11.6 31.5 %copy-start.103 = (f32[784]{0:T(1024)}, f32[784]{0:T(1024)S(1)}, u32[]{:S(2)}) copy-start(f32[784]{0:T(1024)S(1)} %div.141) | copy-start | bytes 9412
  13.5 29.6 %copy-start.107 = (f32[784]{0:T(1024)}, f32[784]{0:T(1024)S(1)}, u32[]{:S(2)}) copy-start(f32[784]{0:T(1024)S(1)} %rsqrt.50) | copy-start | bytes 9412
  16.0 27.1 %copy-start.100 = (f32[768]{0:T(1024)S(1)}, f32[768]{0:T(1024)}, u32[]{:S(2)}) copy-start(f32[768]{0:T(1024)} %param.33) | copy-start | bytes 9220
  16.1 27.1 %copy-start.114 = (f32[768]{0:T(1024)S(1)}, f32[768]{0:T(1024)}, u32[]{:S(2)}) copy-start(f32[768]{0:T(1024)} %param.34) | copy-start | bytes 9220
  16.1 27.1 %copy-start.123 = (f32[2304]{0:T(1024)S(1)}, f32[2304]{0:T(1024)}, u32[]{:S(2)}) copy-start(f32[2304]{0:T(1024)} %param.36) | copy-start | bytes 27652
  66.2 97.7 %all-to-all-start = ((bf16[16,49,3,4,192]{4,0,2,1,3:T(8,128)(2,1)}), bf16[16,49,3,4,192]{4,0,2,1,3:T(8,128)(2,1)}, u32[]{:S(2)}, u32[]{:S(2)}) async-start(bf16[16,49,3,4,192]{4,0,2,1,3:T(8,128)(2,1)} %copy.325), calls=%async_computation | async-start | bytes 9633792 | tf_op jit(solution)/shard_map/all_to_all | solution.py:229
  71.2 583.8 %all-gather.11.cloned.1.call-start = ((), (), s32[]{:S(2)}) async-start(), calls=%async_computation.15 | async-start | bytes 5898240 | tf_op jit(solution)/shard_map/all_gather | solution.py:192
  100.4 69.2 %copy-start.53 = (f32[14,14,27]{2,1,0:T(8,128)S(1)}, f32[14,14,27]{2,1,0:T(8,128)}, u32[]{:S(2)}) copy-start(f32[14,14,27]{2,1,0:T(8,128)} %constant.109.clone) | copy-start | bytes 63508
  100.4 70.3 %copy-start.99 = (f32[27,64]{1,0:T(8,128)S(1)}, f32[27,64]{1,0:T(8,128)}, u32[]{:S(2)}) copy-start(f32[27,64]{1,0:T(8,128)} %param.38) | copy-start | bytes 20740
  163.9 64.3 %all-to-all-start.2 = ((bf16[16,49,3,4,192]{4,0,2,1,3:T(8,128)(2,1)}), bf16[16,49,3,4,192]{4,0,2,1,3:T(8,128)(2,1)}, u32[]{:S(2)}, u32[]{:S(2)}) async-start(bf16[16,49,3,4,192]{4,0,2,1,3:T(8,128)(2,1)} %copy.345), calls=%async_computation.2 | async-start | bytes 9633792 | tf_op jit(solution)/shard_map/all_to_all | solution.py:229
  169.9 153.0 %copy-start.58 = (f32[14,14,64,1,1]{2,1,4,3,0:T(8,128)}, f32[14,14,64,1,1]{2,1,4,3,0:T(8,128)S(1)}, u32[]{:S(2)}) copy-start(f32[14,14,64,1,1]{2,1,4,3,0:T(8,128)S(1)} %convolution_bitcast_fusion) | copy-start | bytes 150532
  170.0 356.1 %copy-start.85 = (pred[16,196]{1,0:T(8,128)(4,1)}, pred[16,196]{1,0:T(8,128)(4,1)S(1)}, u32[]{:S(2)}) copy-start(pred[16,196]{1,0:T(8,128)(4,1)S(1)} %get-tuple-element.167) | copy-start | bytes 9412
  170.0 356.1 %copy-start.87 = (pred[16,196]{1,0:T(8,128)(4,1)}, pred[16,196]{1,0:T(8,128)(4,1)S(1)}, u32[]{:S(2)}) copy-start(pred[16,196]{1,0:T(8,128)(4,1)S(1)} %get-tuple-element.166) | copy-start | bytes 9412
  171.0 132.9 %copy-start.60 = (f32[14,14,64]{2,1,0:T(8,128)}, f32[14,14,64]{2,1,0:T(8,128)S(1)}, u32[]{:S(2)}) copy-start(f32[14,14,64]{2,1,0:T(8,128)S(1)} %fusion.128) | copy-start | bytes 150532
  208.0 76.6 %copy-start.6 = (bf16[16,196,1,3,64]{4,0,3,1,2:T(8,128)(2,1)}, bf16[16,196,1,3,64]{4,0,3,1,2:T(8,128)(2,1)S(1)}, u32[]{:S(2)}) copy-start(bf16[16,196,1,3,64]{4,0,3,1,2:T(8,128)(2,1)S(1)} %copy.331) | copy-start | bytes 3612676
  265.5 57.4 %copy-start.8 = (bf16[16,196,1,3,64]{4,0,3,1,2:T(8,128)(2,1)}, bf16[16,196,1,3,64]{4,0,3,1,2:T(8,128)(2,1)S(1)}, u32[]{:S(2)}) copy-start(bf16[16,196,1,3,64]{4,0,3,1,2:T(8,128)(2,1)S(1)} %copy.351) | copy-start | bytes 3612676
  347.2 161.6 %copy-start.19 = (bf16[16,196,1,3,64]{1,4,3,0,2:T(8,128)(2,1)}, bf16[16,196,1,3,64]{1,4,3,0,2:T(8,128)(2,1)S(1)}, u32[]{:S(2)}) copy-start(bf16[16,196,1,3,64]{1,4,3,0,2:T(8,128)(2,1)S(1)} %copy.442) | copy-start | bytes 3612676
  377.0 113.1 %copy-start.17 = (bf16[16,196,1,3,64]{1,4,3,0,2:T(8,128)(2,1)}, bf16[16,196,1,3,64]{1,4,3,0,2:T(8,128)(2,1)S(1)}, u32[]{:S(2)}) copy-start(bf16[16,196,1,3,64]{1,4,3,0,2:T(8,128)(2,1)S(1)} %copy.445) | copy-start | bytes 3612676
  496.7 12.2 copy-start.46
  571.3 32.8 %all-to-all-start.3 = ((bf16[16,196,1,192]{3,0,2,1:T(8,128)(2,1)}), bf16[16,196,1,192]{3,0,2,1:T(8,128)(2,1)}, u32[]{:S(2)}, u32[]{:S(2)}) async-start(bf16[16,196,1,192]{3,0,2,1:T(8,128)(2,1)} %copy.359), calls=%async_computation.3 | async-start | bytes 3211264 | tf_op jit(solution)/shard_map/all_to_all | solution.py:232
  604.1 25.0 %all-to-all-start.1 = ((bf16[16,196,1,192]{3,0,2,1:T(8,128)(2,1)}), bf16[16,196,1,192]{3,0,2,1:T(8,128)(2,1)}, u32[]{:S(2)}, u32[]{:S(2)}) async-start(bf16[16,196,1,192]{3,0,2,1:T(8,128)(2,1)} %copy.339), calls=%async_computation.1 | async-start | bytes 3211264 | tf_op jit(solution)/shard_map/all_to_all | solution.py:232
  608.6 721.0 %reduce-scatter.7.cloned.1.call-start = ((), (), s32[]{:S(2)}) async-start(), calls=%async_computation.17 | async-start | bytes 1474560 | tf_op jit(solution)/shard_map/reduce_scatter | solution.py:296
  643.5 79.3 %copy-start.13 = (f32[784,768]{1,0:T(8,128)}, f32[784,768]{1,0:T(8,128)S(1)}, u32[]{:S(2)}) copy-start(f32[784,768]{1,0:T(8,128)S(1)} %get-tuple-element.181) | copy-start | bytes 7225348
  655.1 14.6 copy-start.120
  655.1 20.8 %slice-start.4 = ((s8[9633792]{0:T(1024)(128)(4,1)}), s8[4194304]{0:T(1024)(128)(4,1)S(1)}, s32[]{:S(2)}) async-start(s8[9633792]{0:T(1024)(128)(4,1)} %bitcast.306), calls=%async_computation.24 | async-start | bytes 8388608
  655.1 20.8 %slice-start.5 = ((s8[9633792]{0:T(1024)(128)(4,1)}), s8[4194304]{0:T(1024)(128)(4,1)S(1)}, s32[]{:S(2)}) async-start(s8[9633792]{0:T(1024)(128)(4,1)} %bitcast.306), calls=%async_computation.25 | async-start | bytes 8388608
  669.7 17.7 %slice-start.2 = ((s8[4718592]{0:T(1024)(128)(4,1)}), s8[4194304]{0:T(1024)(128)(4,1)S(1)}, s32[]{:S(2)}) async-start(s8[4718592]{0:T(1024)(128)(4,1)} %bitcast.304), calls=%async_computation.22 | async-start | bytes 8388608
  687.4 15.4 copy-start.38
  722.8 679.3 %reduce-scatter.9.cloned.1.call-start = ((), (), s32[]{:S(2)}) async-start(), calls=%async_computation.18 | async-start | bytes 5898240 | tf_op jit(solution)/shard_map/reduce_scatter | solution.py:299
  761.9 39.5 %all-to-all-start.4 = ((bf16[16,49,4,192]{3,0,1,2:T(8,128)(2,1)}), bf16[16,49,4,192]{3,0,1,2:T(8,128)(2,1)}, u32[]{:S(2)}, u32[]{:S(2)}) async-start(bf16[16,49,4,192]{3,0,1,2:T(8,128)(2,1)} %copy.362), calls=%async_computation.4 | async-start | bytes 3211264 | tf_op jit(solution)/shard_map/all_to_all | solution.py:271
  766.3 635.8 %reduce-scatter.11.cloned.1.call-start = ((), (), s32[]{:S(2)}) async-start(), calls=%async_computation.19 | async-start | bytes 5898240 | tf_op jit(solution)/shard_map/reduce_scatter | solution.py:302
  801.5 115.9 %all-to-all-start.6 = ((bf16[16,49,4,192]{3,0,1,2:T(8,128)(2,1)}), bf16[16,49,4,192]{3,0,1,2:T(8,128)(2,1)S(1)}, u32[]{:S(2)}, u32[]{:S(2)}) async-start(bf16[16,49,4,192]{3,0,1,2:T(8,128)(2,1)} %copy.382), calls=%async_computation.6 | async-start | bytes 3211264 | tf_op jit(solution)/shard_map/all_to_all | solution.py:271
  825.0 12.4 copy-start.65
  825.0 12.4 copy-start.88
  837.4 62.2 %copy-start.78 = (f32[14,196,1,1]{1,0,3,2:T(8,128)S(1)}, f32[14,196,1,1]{1,0,3,2:T(8,128)}, u32[]{:S(2)}) copy-start(f32[14,196,1,1]{1,0,3,2:T(8,128)} %constant.114) | copy-start | bytes 32932
  899.6 13.5 copy-start.3
  1023.1 169.4 %all-to-all-start.5 = ((bf16[16,196,3,1,192]{4,0,2,3,1:T(8,128)(2,1)}), bf16[16,196,3,1,192]{4,0,2,3,1:T(8,128)(2,1)}, u32[]{:S(2)}, u32[]{:S(2)}) async-start(bf16[16,196,3,1,192]{4,0,2,3,1:T(8,128)(2,1)} %pad_maximum_fusion), calls=%async_computation.5 | async-start | bytes 9633792 | tf_op jit(solution)/shard_map/all_to_all | solution.py:280
  1028.1 12.1 copy-start.63
  1040.3 62.0 %copy-start.45 = (bf16[16,196,1,3,64]{1,4,3,0,2:T(8,128)(2,1)S(1)}, bf16[16,196,1,3,64]{1,4,3,0,2:T(8,128)(2,1)}, u32[]{:S(2)}) copy-start(bf16[16,196,1,3,64]{1,4,3,0,2:T(8,128)(2,1)} %copy.444) | copy-start | bytes 3612676
  1192.5 60.0 %all-to-all-start.7 = ((bf16[16,196,3,1,192]{4,0,2,3,1:T(8,128)(2,1)}), bf16[16,196,3,1,192]{4,0,2,3,1:T(8,128)(2,1)}, u32[]{:S(2)}, u32[]{:S(2)}) async-start(bf16[16,196,3,1,192]{4,0,2,3,1:T(8,128)(2,1)} %pad_maximum_fusion.1), calls=%async_computation.7 | async-start | bytes 9633792 | tf_op jit(solution)/shard_map/all_to_all | solution.py:280
  1197.7 204.4 %reduce-scatter.5.cloned.1.call-start = ((), (), s32[]{:S(2)}) async-start(), calls=%async_computation.16 | async-start | bytes 4423680 | tf_op jit(solution)/shard_map/reduce_scatter | solution.py:293
  1308.9 15.2 slice-start
  1358.2 43.9 %copy-start.76 = (bf16[192,768]{1,0:T(8,128)(2,1)S(1)}, bf16[192,768]{1,0:T(8,128)(2,1)}, u32[]{:S(2)}) copy-start(bf16[192,768]{1,0:T(8,128)(2,1)} %reduce-scatter.7.cloned.1.call-done) | copy-start | bytes 884740
  1358.2 321.0 %copy-start.1 = (f32[27,64]{1,0:T(8,128)S(1)}, f32[27,64]{1,0:T(8,128)}, u32[]{:S(2)}) copy-start(f32[27,64]{1,0:T(8,128)} %param.37) | copy-start | bytes 20740
  (104 other events, 533.7 us)
Sparse Core Ops, SparseCore 0:
  9.6 33.4 all-gather.4
  44.7 17.4 all-gather.6
  63.7 62.7 all-gather.8
  127.9 54.3 all-gather.10
  722.9 25.7 reduce-scatter.6
  751.2 65.3 reduce-scatter.8
  819.1 47.8 reduce-scatter.10
  1280.9 40.6 reduce-scatter.4
where the time goes:
time: 1700 us; the launch traced here: 1690 us
  local copies, waits for them, and re-layouts  505 us (30%)
  matrix products  449 us (26%)
  blocking collectives  319 us (19%)
  other arithmetic  219 us (13%)
  waiting for transfers between devices  140 us (8%)
  starting transfers between devices  38.1 us (2%)
    psum x1, blocking collectives, local(): lax.psum((shares[0], shares[1], shares[2], shares[3]), ('dp', 'seq'))  277 us
    sub x2, other arithmetic, attend_back(): grad_soft - jnp.sum(soft_weights * grad_soft, axis=-1, keepdims=True)  124 us
    all_to_all x2, waiting for transfers between devices, local(): lax.all_to_all(triple, 'tensor', split_axis=3, concat_axis=1, tiled=True)  83.6 us
    dot_general x8, matrix products, times_transposed(): lax.dot_general(left, weight, (((1,), (1,)), ((), ())), preferred_element...  62.5 us
    dot_general x8, matrix products, contract_rows(): lax.dot_general(left, right, (((0,), (0,)), ((), ())), preferred_element_...  47.9 us
    unnamed x280, local copies, waits for them, and re-layouts  45.3 us
    reshape x6, local copies, waits for them, and re-layouts, attend_back(): grad_width.reshape(slab_count, heads_dev, window, window, window)  44.9 us
    psum x1, blocking collectives, local(): lax.psum((sums[0], sums[1], sums[3], sums[4], sums[5], sums[7], sums[8],...  41.9 us
  transfers between devices with their start and end apart: 16, of which 6 were waited for; matrix products, arithmetic and copies ran while one was open for 65% of the time, Pallas kernels for 0%

commit v1 on v0

--- a/solution.py
+++ b/solution.py
@@ -309,19 +309,22 @@
     expand_gradient = blocks[2]
     shrink_gradient = blocks[3]
     small = lax.psum(
-        (
-            sums[0],
-            sums[1],
-            sums[3],
-            sums[4],
-            sums[5],
-            sums[7],
-            sums[8],
-            sums[9],
-            sums[11],
-            sums[13],
+        lax.psum(
+            (
+                sums[0],
+                sums[1],
+                sums[3],
+                sums[4],
+                sums[5],
+                sums[7],
+                sums[8],
+                sums[9],
+                sums[11],
+                sums[13],
+            ),
+            "dp",
         ),
-        ("dp", "seq", "tensor"),
+        ("seq", "tensor"),
     )
     result = jnp.stack(results, axis=0)
     tokens_gradient = jnp.stack(input_grads, axis=0)

time: 1700 us -> 1720 us (1.012)
  blocking collectives: 319 us -> 342 us
    psum x0 -> x1, blocking collectives: none -> 59.4 us  [local(): lax.psum(lax.psum((sums[0], sums[1], sums[3], sums[4], sums[5], sums[7],...]
    psum x1, blocking collectives: 41.9 us -> 9.77 us  [local(): lax.psum((sums[0], sums[1], sums[3], sums[4], sums[5], sums[7], sums[8],...]
  transfers between devices with their start and end apart: 16 -> 16, of which waited for: 6 -> 6; matrix products, arithmetic and copies ran while one was open for 65% -> 64% of each run, Pallas kernels for 0% -> 0%
where the time goes in v1:
time: 1720 us; the launch traced here: 1710 us
  local copies, waits for them, and re-layouts  505 us (29%)
  matrix products  449 us (26%)
  blocking collectives  342 us (20%)
  other arithmetic  219 us (13%)
  waiting for transfers between devices  140 us (8%)
  starting transfers between devices  38.1 us (2%)
    psum x1, blocking collectives, local(): lax.psum((shares[0], shares[1], shares[2], shares[3]), ('dp', 'seq'))  272 us
    sub x2, other arithmetic, attend_back(): grad_soft - jnp.sum(soft_weights * grad_soft, axis=-1, keepdims=True)  124 us
    all_to_all x2, waiting for transfers between devices, local(): lax.all_to_all(triple, 'tensor', split_axis=3, concat_axis=1, tiled=True)  83.7 us
    dot_general x8, matrix products, times_transposed(): lax.dot_general(left, weight, (((1,), (1,)), ((), ())), preferred_element...  62.5 us
    psum x1, blocking collectives, local(): lax.psum(lax.psum((sums[0], sums[1], sums[3], sums[4], sums[5], sums[7],...  59.4 us
    dot_general x8, matrix products, contract_rows(): lax.dot_general(left, right, (((0,), (0,)), ((), ())), preferred_element_...  48 us
    unnamed x280, local copies, waits for them, and re-layouts  45.3 us
    reshape x6, local copies, waits for them, and re-layouts, attend_back(): grad_width.reshape(slab_count, heads_dev, window, window, window)  44.8 us
  transfers between devices with their start and end apart: 16, of which 6 were waited for; matrix products, arithmetic and copies ran while one was open for 64% of the time, Pallas kernels for 0%

profile of v1, /device:TPU:0, one launch (start us, length us, event | category | flops | bytes accessed | tf_op | source)
XLA Modules:
  0.0 1708.8 jit_solution(1974956566056886688)
XLA Ops:
  17.8 25.4 %all-gather.5.cloned.1.call-done = bf16[768,2304]{1,0:T(8,128)(2,1)} async-done(((bf16[192,2304]{1,0:T(8,128)(2,1)}), bf16[768,2304]{1,0:T(8,128)(2,1)}) %all-gather.5.cloned.1.call-update) | async-done | bytes 3538960 | tf_op jit(solution)/shard_map/all_gather | solution.py:189
  50.9 10.1 reshape.1058
  85.2 10.1 reshape.1065
  100.4 63.5 %all-to-all-done = bf16[16,49,3,4,192]{4,0,2,1,3:T(8,128)(2,1)} async-done(((bf16[16,49,3,4,192]{4,0,2,1,3:T(8,128)(2,1)}), bf16[16,49,3,4,192]{4,0,2,1,3:T(8,128)(2,1)}, u32[]{:S(2)}, u32[]{:S(2)}) %all-to-all-start) | async-done | bytes 3612704 | tf_op jit(solution)/shard_map/all_to_all | solution.py:229
  170.9 18.2 %reshape.1102 = bf16[16,196,3,3,64]{4,3,0,2,1:T(4,128)(2,1)} reshape(bf16[16,4,49,3,1,192]{5,0,3,2,1,4:T(8,128)(2,1)} %bitcast.1) | data formatting | bytes 7225344 | tf_op jit(solution)/shard_map/reshape | solution.py:230
  189.2 10.0 fusion.166
  208.0 20.2 %all-to-all-done.2 = bf16[16,49,3,4,192]{4,0,2,1,3:T(8,128)(2,1)} async-done(((bf16[16,49,3,4,192]{4,0,2,1,3:T(8,128)(2,1)}), bf16[16,49,3,4,192]{4,0,2,1,3:T(8,128)(2,1)}, u32[]{:S(2)}, u32[]{:S(2)}) %all-to-all-start.2) | async-done | bytes 3612704 | tf_op jit(solution)/shard_map/all_to_all | solution.py:229
  228.2 18.2 %reshape.1104 = bf16[16,196,3,3,64]{4,3,0,2,1:T(4,128)(2,1)} reshape(bf16[16,4,49,3,1,192]{5,0,3,2,1,4:T(8,128)(2,1)} %bitcast.25) | data formatting | bytes 7225344 | tf_op jit(solution)/shard_map/reshape | solution.py:230
  246.4 10.8 fusion.167
  265.5 19.0 %fusion.52 = f32[16,3,14,14,14]{0,4,1,2,3:T(8,128)} fusion(bf16[16,14,14,3,64]{4,0,3,2,1:T(8,128)(2,1)S(1)} %bitcast.281, f32[14,14,64]{2,1,0:T(8,128)S(1)} %fusion.128), kind=kOutput, calls=%fused_computation.124 | convolution fusion | flops 101154816 | bytes 1781248 | tf_op jit(solution)/shard_map/sijhc,jlc->shijl/dot_general | solution.py:77
  284.5 19.2 %fusion.170 = f32[14,14,16,14,3]{2,1,4,3,0:T(8,128)} fusion(f32[14,14,64,1,1]{2,1,4,3,0:T(8,128)S(1)} %convolution_bitcast_fusion, bf16[16,14,14,3,64]{4,0,3,2,1:T(8,128)(2,1)S(1)} %bitcast.282), kind=kOutput, calls=%fused_computation.272 | convolution fusion | flops 101154816 | bytes 1781248 | tf_op jit(solution)/shard_map/sijhc,ikc->shijk/dot_general | solution.py:76
  303.8 19.1 %fusion.55 = f32[16,3,14,14,14]{0,4,1,2,3:T(8,128)} fusion(bf16[16,14,14,3,64]{4,0,3,2,1:T(8,128)(2,1)S(1)} %bitcast.285, f32[14,14,64]{2,1,0:T(8,128)S(1)} %fusion.128), kind=kOutput, calls=%fused_computation.125 | convolution fusion | flops 101154816 | bytes 1781248 | tf_op jit(solution)/shard_map/sijhc,jlc->shijl/dot_general | solution.py:77
  322.8 19.4 %fusion.173 = f32[14,14,16,14,3]{2,1,4,3,0:T(8,128)} fusion(f32[14,14,64,1,1]{2,1,4,3,0:T(8,128)S(1)} %convolution_bitcast_fusion, bf16[16,14,14,3,64]{4,0,3,2,1:T(8,128)(2,1)S(1)} %bitcast.286), kind=kOutput, calls=%fused_computation.275 | convolution fusion | flops 101154816 | bytes 1781248 | tf_op jit(solution)/shard_map/sijhc,ikc->shijk/dot_general | solution.py:76
  347.1 9.8 copy.430
  377.0 9.8 copy.435
  396.3 11.4 fusion.174
  407.8 12.1 copy.353
  419.8 11.3 fusion.175
  431.1 12.0 copy.357
  443.2 11.3 fusion.171
  454.4 12.2 copy.333
  466.7 11.4 fusion.172
  478.0 12.1 copy.337
  496.7 12.2 copy.350
  514.0 12.0 copy.330
  526.0 26.2 %fusion.164 = (f32[16,3,196]{0,2,1:T(8,128)S(1)}, f32[16,3,196,196]{3,0,2,1:T(8,128)}, f32[16,3,196]{0,2,1:T(8,128)S(1)}, f32[16,3,196,196]{3,0,2,1:T(8,128)}) fusion(f32[16,3,196,196]{3,0,2,1:T(8,128)} %copy.337, f32[16,3,196,196]{3,0,2,1:T(8,128)} %copy.333, f32[16,3,196,196]{3,0,2,1:T(8,128)} %copy.330, pred[16,196]{1,0:T(8,128)(4,1)S(1)} %get-tuple-element.176, ...), kind=kLoop, calls=%fused_computation.266 | loop fusion | flops 18420864 | bytes 59088512 | tf_op jit(solution)/shard_map/reduce_max | solution.py:90
  581.4 9.5 fusion.6
  644.3 10.7 fusion.159
  655.1 14.6 convert_reduce_fusion
  675.9 11.5 multiply_convert_fusion.1
  687.4 15.4 convert_reduce_fusion.1
  702.9 9.4 multiply_reduce_fusion.3
  730.7 9.5 add_convert_fusion.3
  825.1 12.4 copy.365
  837.5 62.1 %select_convert_fusion.1 = bf16[16,3,196,196]{3,0,2,1:T(8,128)(2,1)S(1)} fusion(f32[16,3,196,196]{3,0,2,1:T(8,128)} %copy.365, f32[16,3,196,196]{3,0,2,1:T(8,128)} %get-tuple-element.135, f32[16,3,196]{0,2,1:T(8,128)S(1)} %copy-done.65, pred[16,196]{1,0:T(8,128)(4,1)S(1)} %copy-done.88), kind=kOutput, calls=%fused_computation.11 | output fusion | flops 12917379 | bytes 18480448 | tf_op jit(solution)/shard_map/sub | solution.py:123
  966.4 11.5 fusion.176
  1028.2 12.1 copy.385
  1040.3 62.0 %select_convert_fusion = bf16[16,3,196,196]{3,0,2,1:T(8,128)(2,1)S(1)} fusion(f32[16,3,196,196]{3,0,2,1:T(8,128)} %copy.385, f32[16,3,196,196]{3,0,2,1:T(8,128)} %get-tuple-element.202, f32[16,3,196]{0,2,1:T(8,128)S(1)} %copy-done.63, pred[16,196]{1,0:T(8,128)(4,1)S(1)} %copy-done.86), kind=kOutput, calls=%fused_computation.6 | output fusion | flops 12917379 | bytes 18480448 | tf_op jit(solution)/shard_map/sub | solution.py:123
  1152.6 10.1 fusion.178
  1210.7 8.7 add_convert_fusion.14
  1230.5 8.9 reshape.1077
  1239.4 13.0 all-to-all-done.7
  1259.5 9.4 reshape.1083
  1289.4 9.4 copy.410
  1298.9 9.6 copy.412
  1360.0 9.8 all-reduce.2
  1369.8 59.4 %all-reduce = (f32[768]{0:T(1024)}, f32[768]{0:T(1024)}, f32[2304]{0:T(1024)}, f32[27,64]{1,0:T(8,128)}, f32[27,64]{1,0:T(8,128)}, /*index=5*/f32[768]{0:T(1024)...) all-reduce(f32[768]{0:T(1024)S(1)} %get-tuple-element.112, ...), channel_id=1, replica_groups=mesh['dp'=2,'seq'=4,'tensor'=4] {'seq','tensor'}, use_global_device_ids=true, to_apply=%region_25.26 | all-reduce | flops 13440 | bytes 107520 | tf_op jit(solution)/shard_map/psum | solution.py:311
  1429.2 272.5 %all-reduce.4 = (f32[192,2304]{1,0:T(8,128)}, f32[192,768]{1,0:T(8,128)}, f32[192,3072]{1,0:T(8,128)}, f32[768,768]{1,0:T(8,128)}) all-reduce(bf16[192,2304]{1,0:T(8,128)(2,1)} %reduce-scatter.5.cloned.1.call-done, bf16[192,768]{1,0:T(8,128)(2,1)S(1)} %copy-done.76, ...), channel_id=1, replica_groups=mesh['dp'=2,'seq'=4,'tensor'=4] {'dp','seq'}, use_global_device_ids=true, to_apply=%region_31.32 | all-reduce | flops 1769472 | bytes 10616832 | tf_op jit(solution)/shard_map/psum | solution.py:306
  (514 shorter events, 613.8 us)
Async XLA Ops:
  7.2 162.4 %copy-start = (f32[27,64]{1,0:T(8,128)S(1)}, f32[27,64]{1,0:T(8,128)}, u32[]{:S(2)}) copy-start(f32[27,64]{1,0:T(8,128)} %param.37) | copy-start | bytes 20740
  7.2 35.9 %all-gather.5.cloned.1.call-start = ((), (), s32[]{:S(2)}) async-start(), calls=%async_computation.12 | async-start | bytes 4423680 | tf_op jit(solution)/shard_map/all_gather | solution.py:189
  7.9 628.7 %all-gather.7.cloned.1.call-start = ((), (), s32[]{:S(2)}) async-start(), calls=%async_computation.13 | async-start | bytes 1474560 | tf_op jit(solution)/shard_map/all_gather | solution.py:190
  8.7 635.4 %all-gather.9.cloned.1.call-start = ((), (), s32[]{:S(2)}) async-start(), calls=%async_computation.14 | async-start | bytes 5898240 | tf_op jit(solution)/shard_map/all_gather | solution.py:191
  11.6 31.5 %copy-start.103 = (f32[784]{0:T(1024)}, f32[784]{0:T(1024)S(1)}, u32[]{:S(2)}) copy-start(f32[784]{0:T(1024)S(1)} %div.141) | copy-start | bytes 9412
  13.5 29.6 %copy-start.107 = (f32[784]{0:T(1024)}, f32[784]{0:T(1024)S(1)}, u32[]{:S(2)}) copy-start(f32[784]{0:T(1024)S(1)} %rsqrt.50) | copy-start | bytes 9412
  16.0 27.1 %copy-start.100 = (f32[768]{0:T(1024)S(1)}, f32[768]{0:T(1024)}, u32[]{:S(2)}) copy-start(f32[768]{0:T(1024)} %param.33) | copy-start | bytes 9220
  16.1 27.1 %copy-start.114 = (f32[768]{0:T(1024)S(1)}, f32[768]{0:T(1024)}, u32[]{:S(2)}) copy-start(f32[768]{0:T(1024)} %param.34) | copy-start | bytes 9220
  16.1 27.1 %copy-start.123 = (f32[2304]{0:T(1024)S(1)}, f32[2304]{0:T(1024)}, u32[]{:S(2)}) copy-start(f32[2304]{0:T(1024)} %param.36) | copy-start | bytes 27652
  66.2 97.7 %all-to-all-start = ((bf16[16,49,3,4,192]{4,0,2,1,3:T(8,128)(2,1)}), bf16[16,49,3,4,192]{4,0,2,1,3:T(8,128)(2,1)}, u32[]{:S(2)}, u32[]{:S(2)}) async-start(bf16[16,49,3,4,192]{4,0,2,1,3:T(8,128)(2,1)} %copy.325), calls=%async_computation | async-start | bytes 9633792 | tf_op jit(solution)/shard_map/all_to_all | solution.py:229
  71.2 583.8 %all-gather.11.cloned.1.call-start = ((), (), s32[]{:S(2)}) async-start(), calls=%async_computation.15 | async-start | bytes 5898240 | tf_op jit(solution)/shard_map/all_gather | solution.py:192
  100.4 69.2 %copy-start.53 = (f32[14,14,27]{2,1,0:T(8,128)S(1)}, f32[14,14,27]{2,1,0:T(8,128)}, u32[]{:S(2)}) copy-start(f32[14,14,27]{2,1,0:T(8,128)} %constant.109.clone) | copy-start | bytes 63508
  100.4 70.3 %copy-start.99 = (f32[27,64]{1,0:T(8,128)S(1)}, f32[27,64]{1,0:T(8,128)}, u32[]{:S(2)}) copy-start(f32[27,64]{1,0:T(8,128)} %param.38) | copy-start | bytes 20740
  163.9 64.3 %all-to-all-start.2 = ((bf16[16,49,3,4,192]{4,0,2,1,3:T(8,128)(2,1)}), bf16[16,49,3,4,192]{4,0,2,1,3:T(8,128)(2,1)}, u32[]{:S(2)}, u32[]{:S(2)}) async-start(bf16[16,49,3,4,192]{4,0,2,1,3:T(8,128)(2,1)} %copy.345), calls=%async_computation.2 | async-start | bytes 9633792 | tf_op jit(solution)/shard_map/all_to_all | solution.py:229
  169.8 153.0 %copy-start.58 = (f32[14,14,64,1,1]{2,1,4,3,0:T(8,128)}, f32[14,14,64,1,1]{2,1,4,3,0:T(8,128)S(1)}, u32[]{:S(2)}) copy-start(f32[14,14,64,1,1]{2,1,4,3,0:T(8,128)S(1)} %convolution_bitcast_fusion) | copy-start | bytes 150532
  170.0 356.1 %copy-start.85 = (pred[16,196]{1,0:T(8,128)(4,1)}, pred[16,196]{1,0:T(8,128)(4,1)S(1)}, u32[]{:S(2)}) copy-start(pred[16,196]{1,0:T(8,128)(4,1)S(1)} %get-tuple-element.177) | copy-start | bytes 9412
  170.0 356.1 %copy-start.87 = (pred[16,196]{1,0:T(8,128)(4,1)}, pred[16,196]{1,0:T(8,128)(4,1)S(1)}, u32[]{:S(2)}) copy-start(pred[16,196]{1,0:T(8,128)(4,1)S(1)} %get-tuple-element.176) | copy-start | bytes 9412
  170.9 132.8 %copy-start.60 = (f32[14,14,64]{2,1,0:T(8,128)}, f32[14,14,64]{2,1,0:T(8,128)S(1)}, u32[]{:S(2)}) copy-start(f32[14,14,64]{2,1,0:T(8,128)S(1)} %fusion.128) | copy-start | bytes 150532
  208.0 76.5 %copy-start.6 = (bf16[16,196,1,3,64]{4,0,3,1,2:T(8,128)(2,1)}, bf16[16,196,1,3,64]{4,0,3,1,2:T(8,128)(2,1)S(1)}, u32[]{:S(2)}) copy-start(bf16[16,196,1,3,64]{4,0,3,1,2:T(8,128)(2,1)S(1)} %copy.331) | copy-start | bytes 3612676
  265.5 57.4 %copy-start.8 = (bf16[16,196,1,3,64]{4,0,3,1,2:T(8,128)(2,1)}, bf16[16,196,1,3,64]{4,0,3,1,2:T(8,128)(2,1)S(1)}, u32[]{:S(2)}) copy-start(bf16[16,196,1,3,64]{4,0,3,1,2:T(8,128)(2,1)S(1)} %copy.351) | copy-start | bytes 3612676
  347.1 161.7 %copy-start.19 = (bf16[16,196,1,3,64]{1,4,3,0,2:T(8,128)(2,1)}, bf16[16,196,1,3,64]{1,4,3,0,2:T(8,128)(2,1)S(1)}, u32[]{:S(2)}) copy-start(bf16[16,196,1,3,64]{1,4,3,0,2:T(8,128)(2,1)S(1)} %copy.442) | copy-start | bytes 3612676
  377.0 113.1 %copy-start.17 = (bf16[16,196,1,3,64]{1,4,3,0,2:T(8,128)(2,1)}, bf16[16,196,1,3,64]{1,4,3,0,2:T(8,128)(2,1)S(1)}, u32[]{:S(2)}) copy-start(bf16[16,196,1,3,64]{1,4,3,0,2:T(8,128)(2,1)S(1)} %copy.445) | copy-start | bytes 3612676
  496.7 12.2 copy-start.46
  571.3 32.8 %all-to-all-start.3 = ((bf16[16,196,1,192]{3,0,2,1:T(8,128)(2,1)}), bf16[16,196,1,192]{3,0,2,1:T(8,128)(2,1)}, u32[]{:S(2)}, u32[]{:S(2)}) async-start(bf16[16,196,1,192]{3,0,2,1:T(8,128)(2,1)} %copy.359), calls=%async_computation.3 | async-start | bytes 3211264 | tf_op jit(solution)/shard_map/all_to_all | solution.py:232
  604.0 25.0 %all-to-all-start.1 = ((bf16[16,196,1,192]{3,0,2,1:T(8,128)(2,1)}), bf16[16,196,1,192]{3,0,2,1:T(8,128)(2,1)}, u32[]{:S(2)}, u32[]{:S(2)}) async-start(bf16[16,196,1,192]{3,0,2,1:T(8,128)(2,1)} %copy.339), calls=%async_computation.1 | async-start | bytes 3211264 | tf_op jit(solution)/shard_map/all_to_all | solution.py:232
  608.6 720.9 %reduce-scatter.7.cloned.1.call-start = ((), (), s32[]{:S(2)}) async-start(), calls=%async_computation.17 | async-start | bytes 1474560 | tf_op jit(solution)/shard_map/reduce_scatter | solution.py:296
  643.5 79.3 %copy-start.13 = (f32[784,768]{1,0:T(8,128)}, f32[784,768]{1,0:T(8,128)S(1)}, u32[]{:S(2)}) copy-start(f32[784,768]{1,0:T(8,128)S(1)} %get-tuple-element.191) | copy-start | bytes 7225348
  655.1 14.6 copy-start.120
  655.1 20.8 %slice-start.4 = ((s8[9633792]{0:T(1024)(128)(4,1)}), s8[4194304]{0:T(1024)(128)(4,1)S(1)}, s32[]{:S(2)}) async-start(s8[9633792]{0:T(1024)(128)(4,1)} %bitcast.306), calls=%async_computation.24 | async-start | bytes 8388608
  655.1 20.8 %slice-start.5 = ((s8[9633792]{0:T(1024)(128)(4,1)}), s8[4194304]{0:T(1024)(128)(4,1)S(1)}, s32[]{:S(2)}) async-start(s8[9633792]{0:T(1024)(128)(4,1)} %bitcast.306), calls=%async_computation.25 | async-start | bytes 8388608
  669.7 17.7 %slice-start.2 = ((s8[4718592]{0:T(1024)(128)(4,1)}), s8[4194304]{0:T(1024)(128)(4,1)S(1)}, s32[]{:S(2)}) async-start(s8[4718592]{0:T(1024)(128)(4,1)} %bitcast.304), calls=%async_computation.22 | async-start | bytes 8388608
  687.4 15.4 copy-start.38
  722.8 706.4 %reduce-scatter.9.cloned.1.call-start = ((), (), s32[]{:S(2)}) async-start(), calls=%async_computation.18 | async-start | bytes 5898240 | tf_op jit(solution)/shard_map/reduce_scatter | solution.py:299
  761.9 39.6 %all-to-all-start.4 = ((bf16[16,49,4,192]{3,0,1,2:T(8,128)(2,1)}), bf16[16,49,4,192]{3,0,1,2:T(8,128)(2,1)}, u32[]{:S(2)}, u32[]{:S(2)}) async-start(bf16[16,49,4,192]{3,0,1,2:T(8,128)(2,1)} %copy.362), calls=%async_computation.4 | async-start | bytes 3211264 | tf_op jit(solution)/shard_map/all_to_all | solution.py:271
  766.3 662.9 %reduce-scatter.11.cloned.1.call-start = ((), (), s32[]{:S(2)}) async-start(), calls=%async_computation.19 | async-start | bytes 5898240 | tf_op jit(solution)/shard_map/reduce_scatter | solution.py:302
  801.5 115.9 %all-to-all-start.6 = ((bf16[16,49,4,192]{3,0,1,2:T(8,128)(2,1)}), bf16[16,49,4,192]{3,0,1,2:T(8,128)(2,1)S(1)}, u32[]{:S(2)}, u32[]{:S(2)}) async-start(bf16[16,49,4,192]{3,0,1,2:T(8,128)(2,1)} %copy.382), calls=%async_computation.6 | async-start | bytes 3211264 | tf_op jit(solution)/shard_map/all_to_all | solution.py:271
  825.1 12.4 copy-start.65
  825.1 12.4 copy-start.88
  837.5 62.1 %copy-start.78 = (f32[14,196,1,1]{1,0,3,2:T(8,128)S(1)}, f32[14,196,1,1]{1,0,3,2:T(8,128)}, u32[]{:S(2)}) copy-start(f32[14,196,1,1]{1,0,3,2:T(8,128)} %constant.114) | copy-start | bytes 32932
  899.6 13.5 copy-start.3
  1023.1 169.3 %all-to-all-start.5 = ((bf16[16,196,3,1,192]{4,0,2,3,1:T(8,128)(2,1)}), bf16[16,196,3,1,192]{4,0,2,3,1:T(8,128)(2,1)}, u32[]{:S(2)}, u32[]{:S(2)}) async-start(bf16[16,196,3,1,192]{4,0,2,3,1:T(8,128)(2,1)} %pad_maximum_fusion), calls=%async_computation.5 | async-start | bytes 9633792 | tf_op jit(solution)/shard_map/all_to_all | solution.py:280
  1028.1 12.1 copy-start.63
  1040.3 62.0 %copy-start.45 = (bf16[16,196,1,3,64]{1,4,3,0,2:T(8,128)(2,1)S(1)}, bf16[16,196,1,3,64]{1,4,3,0,2:T(8,128)(2,1)}, u32[]{:S(2)}) copy-start(bf16[16,196,1,3,64]{1,4,3,0,2:T(8,128)(2,1)} %copy.444) | copy-start | bytes 3612676
  1192.5 60.0 %all-to-all-start.7 = ((bf16[16,196,3,1,192]{4,0,2,3,1:T(8,128)(2,1)}), bf16[16,196,3,1,192]{4,0,2,3,1:T(8,128)(2,1)}, u32[]{:S(2)}, u32[]{:S(2)}) async-start(bf16[16,196,3,1,192]{4,0,2,3,1:T(8,128)(2,1)} %pad_maximum_fusion.1), calls=%async_computation.7 | async-start | bytes 9633792 | tf_op jit(solution)/shard_map/all_to_all | solution.py:280
  1197.6 231.6 %reduce-scatter.5.cloned.1.call-start = ((), (), s32[]{:S(2)}) async-start(), calls=%async_computation.16 | async-start | bytes 4423680 | tf_op jit(solution)/shard_map/reduce_scatter | solution.py:293
  1308.8 15.2 slice-start
  1358.1 71.1 %copy-start.76 = (bf16[192,768]{1,0:T(8,128)(2,1)S(1)}, bf16[192,768]{1,0:T(8,128)(2,1)}, u32[]{:S(2)}) copy-start(bf16[192,768]{1,0:T(8,128)(2,1)} %reduce-scatter.7.cloned.1.call-done) | copy-start | bytes 884740
  1358.1 343.6 %copy-start.1 = (f32[27,64]{1,0:T(8,128)S(1)}, f32[27,64]{1,0:T(8,128)}, u32[]{:S(2)}) copy-start(f32[27,64]{1,0:T(8,128)} %param.37) | copy-start | bytes 20740
  (104 other events, 533.6 us)
Sparse Core Ops, SparseCore 0:
  9.6 33.4 all-gather.4
  44.7 17.4 all-gather.6
  63.7 62.7 all-gather.8
  127.9 54.4 all-gather.10
  722.9 25.7 reduce-scatter.6
  751.2 65.3 reduce-scatter.8
  819.2 47.8 reduce-scatter.10
  1280.8 40.6 reduce-scatter.4
